TPU v7x, 128 devices: a whole 4x4x4 slice. The times are simulated.
128 devices in a mesh: grp: 4 (over x_hi, core), vec: 32 (over z, y, x_lo).
Axes of the slice: x: 4 (x_hi: 2, x_lo: 2; x = x_hi * 2 + x_lo), y: 4, z: 4, core: 2. Of those that a mesh axis runs over, the one named last changes fastest.
Arguments:
- vv_vectors: bfloat16 [1280, 1000, 1000], P(('grp', 'vec')), may hold values from -0.1875 to 0.1875
- oo_vectors: bfloat16 [1280, 100, 100], P(('grp', 'vec')), may hold values from -0.625 to 0.625
- ov_slab: bfloat16 [1280, 1024], P(('grp', 'vec')), may hold values from -0.15625 to 0.15625
- amplitudes: bfloat16 [100, 1000], P('grp'), may hold values from -6 to 6
Outputs:
- sigma_slab: float32 [96000, 1024], P(('grp', 'vec'))
All inputs are finite; a program needn't handle non-finite values.
Results may differ from a plain program's by a relative error of at most 0.0029.
Values may be sent and summed in bfloat16 or wider, within the bound.
No kernel may reach another device: no remote copies, remote signals or barrier semaphores. Data moves between devices by JAX's collectives and lax.ppermute only.
A program may use at most 128 MiB of HBM per device.

v0:
```python
import jax
import jax.numpy as jnp
from jax import lax
from jax.sharding import PartitionSpec as P

NV = 1000
I_ROWS = 96


def laid_out(blocks, dim):
    dims = list(blocks.shape[1:])
    dims[dim] *= blocks.shape[0]
    return jnp.moveaxis(blocks, 0, dim).reshape(dims)


def from_everyone(array, axis):
    size = lax.axis_size(axis)
    return lax.all_to_all(
        jnp.broadcast_to(array[None], (size, *array.shape)), axis, 0, 0, tiled=True
    )


def collect(array, axis, dim):
    return laid_out(from_everyone(array, axis), dim)


def split_up(array, dim, size):
    dims = array.shape
    blocks = array.reshape(*dims[:dim], size, dims[dim] // size, *dims[dim + 1 :])
    return jnp.moveaxis(blocks, dim, 0)


def joined_exchange(array, axis, axes, splits, concats):
    sizes = [lax.axis_size(a) for a in axes]
    blocks = split_up(array, splits[0], sizes[0])
    blocks = jnp.moveaxis(split_up(blocks, splits[1] + 1, sizes[1]), 0, 1)
    inside = blocks.shape[2:]
    blocks = blocks.reshape(-1, *inside)
    blocks = lax.all_to_all(blocks, axis, split_axis=0, concat_axis=0, tiled=True)
    blocks = laid_out(blocks.reshape(*sizes, *inside), concats[0] + 1)
    return laid_out(blocks, concats[1])


def shards(vv_vectors, oo_vectors, ov_slab, amplitudes):
    amps_all = collect(amplitudes, "grp", 0)
    window = amps_all[:I_ROWS]
    local_count = vv_vectors.shape[0]
    direct_term = jnp.einsum("ib,pab->pia", window, vv_vectors, preferred_element_type=jnp.float32)
    hole_term = jnp.einsum(
        "pji,ja->pia", oo_vectors[:, :, :I_ROWS], amps_all, preferred_element_type=jnp.float32
    )
    dressed = (direct_term - hole_term).astype(jnp.bfloat16).reshape(local_count, I_ROWS * NV)
    regrouped = joined_exchange(dressed, ("grp", "vec"), ("grp", "vec"), (1, 1), (0, 0))
    group_slab = collect(ov_slab, "grp", 0)
    return lax.dot_general(
        regrouped,
        lax.all_gather(group_slab, "vec", axis=0, tiled=True),
        (((0,), (0,)), ((), ())),
        preferred_element_type=jnp.float32,
    )


def solution(mesh):
    return jax.shard_map(
        shards,
        mesh=mesh,
        in_specs=(
            P(("grp", "vec"), None, None),
            P(("grp", "vec"), None, None),
            P(("grp", "vec"), None),
            P("grp", None),
        ),
        out_specs=P(("grp", "vec"), None),
        check_vma=False,
    )
```

profile of v0, /device:TPU:4, one launch (start us, length us, event | category | flops | bytes accessed | tf_op | source)
XLA Modules:
  0.0 197.3 jit_solution(13646007314827454208)
XLA Ops:
  6.5 0.0 all-gather.2.cloned.1.call-start
  6.5 0.8 broadcast_in_dim.5
  7.3 7.6 %all_to_all.15 = bf16[4,10,1024]{2,1,0:T(8,128)(2,1)S(1)} all-to-all(bf16[4,10,1024]{2,1,0:T(8,128)(2,1)S(1)} %broadcast_in_dim.5), channel_id=1, replica_groups=mesh['grp'=4,'vec'=32] {'grp'}, dimensions={0} | all-to-all | bytes 163840 | tf_op jit(solution)/shard_map/all_to_all | solution.py:18
  14.9 0.7 reshape.21
  15.5 0.0 all-gather.2.cloned.1.call-update
  15.6 0.9 broadcast_in_dim.4
  16.4 9.9 %all_to_all.16 = bf16[4,25,1000]{2,1,0:T(8,128)(2,1)S(1)} all-to-all(bf16[4,25,1000]{2,1,0:T(8,128)(2,1)S(1)} %broadcast_in_dim.4), channel_id=1, replica_groups=mesh['grp'=4,'vec'=32] {'grp'}, dimensions={0} | all-to-all | bytes 400000 | tf_op jit(solution)/shard_map/all_to_all | solution.py:18
  26.3 0.1 reshape.17
  26.4 0.1 reshape.23
  26.5 0.0 copy-start
  26.5 10.3 %fusion.2 = f32[10,1000,96]{1,2,0:T(8,128)S(1)} fusion(bf16[10,1000,1000]{2,1,0:T(8,128)(2,1)} %param.4, bf16[100,1000]{1,0:T(8,128)(2,1)S(1)} %reshape.17), kind=kOutput, calls=%fused_computation.4 | convolution fusion | flops 1920000000 | bytes 24036608 | tf_op jit(solution)/shard_map/ib,pab->pia/dot_general | solution.py:48
  36.8 0.0 copy-done
  36.8 0.7 fusion
  37.6 4.3 %reshape_reshape.6 = bf16[10,4,24000]{2,1,0:T(4,128)(2,1)} reshape(bf16[10,96,1000]{2,1,0:T(8,128)(2,1)S(1)} %fusion) | data formatting | bytes 3840000 | tf_op jit(solution)/shard_map/reshape;reshape | solution.py:29
  41.9 6.0 %reshape.18 = bf16[4,10,32,750]{3,2,0,1:T(8,128)(2,1)S(1)} reshape(bf16[4,10,24000]{2,0,1:T(4,128)(2,1)} %bitcast.22) | data formatting | bytes 3840000 | tf_op jit(solution)/shard_map/reshape | solution.py:29
  47.9 1.2 copy.10
  49.1 70.7 %all_to_all.17 = bf16[128,10,750]{2,1,0:T(8,128)(2,1)S(1)} all-to-all(bf16[128,10,750]{2,1,0:T(8,128)(2,1)S(1)} %bitcast.20), channel_id=1, replica_groups=mesh['grp'=4,'vec'=32] {'grp','vec'}, dimensions={0} | all-to-all | bytes 3840000 | tf_op jit(solution)/shard_map/all_to_all | solution.py:39
  119.8 0.4 copy.12
  120.2 2.5 %reshape_reshape.7 = bf16[1280,750]{1,0:T(8,128)(2,1)} reshape(bf16[32,4,10,750]{3,2,1,0:T(8,128)(2,1)S(1)} %copy.12) | data formatting | bytes 3840000 | tf_op jit(solution)/shard_map/reshape;reshape | solution.py:13
  122.7 61.6 %all-gather.2.cloned.1.call-done = bf16[1280,1024]{1,0:T(8,128)(2,1)} async-done(((bf16[40,1024]{1,0:T(8,128)(2,1)}), bf16[1280,1024]{1,0:T(8,128)(2,1)}) %all-gather.2.cloned.1.call-update) | async-done | bytes 2621456 | tf_op jit(solution)/shard_map/all_gather | solution.py:57
  184.3 6.2 %fusion.3 = f32[750,1024]{1,0:T(8,128)} fusion(bf16[1280,750]{1,0:T(8,128)(2,1)} %reshape_reshape.7, bf16[1280,1024]{1,0:T(8,128)(2,1)} %all-gather.2.cloned.1.call-done), kind=kOutput, calls=%fused_computation.5 | convolution fusion | flops 1966080000 | bytes 7613440 | tf_op jit(solution)/shard_map/dot_general | solution.py:55
Async XLA Ops:
  6.5 177.8 %all-gather.2.cloned.1.call-start = ((), (), s32[]{:S(2)}) async-start(), calls=%async_computation.3 | async-start | bytes 2703360 | tf_op jit(solution)/shard_map/all_gather | solution.py:57
  26.5 10.3 %copy-start = (bf16[10,100,100]{2,1,0:T(8,128)(2,1)S(1)}, bf16[10,100,100]{2,1,0:T(8,128)(2,1)}, u32[]{:S(2)}) copy-start(bf16[10,100,100]{2,1,0:T(8,128)(2,1)} %param.5) | copy-start | bytes 600004
Sparse Core Ops, SparseCore 0:
  15.7 168.5 all-gather.1
where the time goes:
time: 198 us; the launch traced here: 197 us
  blocking collectives  88.1 us (44%)
  waiting for transfers between devices  61.6 us (31%)
  matrix products  17.2 us (9%)
  local copies, waits for them, and re-layouts  16.9 us (9%)
  between operations  13.5 us (7%)
    all_to_all x1, blocking collectives, joined_exchange(): lax.all_to_all(blocks, axis, split_axis=0, concat_axis=0, tiled=True)  70.7 us
    all_gather x1, waiting for transfers between devices, shards(): lax.all_gather(group_slab, 'vec', axis=0, tiled=True)  61.6 us
    all_to_all x2, blocking collectives, from_everyone(): lax.all_to_all(jnp.broadcast_to(array[None], (size, *array.shape)), axis,...  17.5 us
    dot_general x1, matrix products, shards(): jnp.einsum('ib,pab->pia', window, vv_vectors, preferred_element_type=jnp....  10.3 us
    reshape x2, local copies, waits for them, and re-layouts, split_up(): array.reshape(*dims[:dim], size, dims[dim] // size, *dims[dim + 1:])  7.22 us
    dot_general x1, matrix products, shards(): lax.dot_general(regrouped, lax.all_gather(group_slab, 'vec', axis=0, tile...  6.16 us
    another operation x1, local copies, waits for them, and re-layouts, split_up(): array.reshape(*dims[:dim], size, dims[dim] // size, *dims[dim + 1:])  4.33 us
  transfers between devices with their start and end apart: 1, of which 1 were waited for; matrix products, arithmetic and copies ran while one was open for 13% of the time, Pallas kernels for 0%

commit v1 on v0

v1 whole, which is shorter than its diff:
```python
import jax
import jax.numpy as jnp
from jax import lax
from jax.experimental import pallas as pl
from jax.experimental.pallas import tpu as pltpu
from jax.sharding import Mesh, PartitionSpec as P

NO = 100
NV = 1000
I_ROWS = 96
SLAB = 1024
DEVICES = 128
LOCAL = 10
QUARTER = 250
BLOCK = 32
WIDE = 256
AXES = ("x_hi", "core", "z", "y", "x_lo")
RING = ("z", "y", "x_hi", "x_lo", "core")
F32 = jnp.float32
BF16 = jnp.bfloat16


def offset_of(piece):
    return (QUARTER * piece) % WIDE


def dress_kernel(vv_ref, oo_ref, amps_ref, out_ref, window, wide, blocks):
    p = pl.program_id(0)
    row = lax.broadcasted_iota(jnp.int32, (I_ROWS, NO), 0)
    col = lax.broadcasted_iota(jnp.int32, (I_ROWS, NO), 1)
    pick = jnp.where(col == 3 * (row % 32) + row // 32, 1.0, 0.0).astype(BF16)

    @pl.when(p == 0)
    def _():
        window[...] = jnp.dot(pick, amps_ref[...], preferred_element_type=F32).astype(BF16)
        wide[...] = jnp.zeros_like(wide)
        blocks[...] = jnp.zeros_like(blocks)

    direct = lax.dot_general(
        window[...], vv_ref[0], (((1,), (1,)), ((), ())), preferred_element_type=F32
    )
    holes = lax.dot_general(
        pick, oo_ref[0], (((1,), (1,)), ((), ())), preferred_element_type=F32
    ).astype(BF16)
    hole = jnp.dot(holes, amps_ref[...], preferred_element_type=F32)
    wide[:, :NV] = direct - hole

    lane = lax.broadcasted_iota(jnp.int32, (32, WIDE), 1)
    for t in range(3):
        for q in range(4):
            block, s = divmod(4 * t + q, 3)
            low = min(QUARTER * q // 128 * 128, 512)
            shift = (offset_of(s) - (QUARTER * q - low)) % 512
            part = wide[32 * t : 32 * (t + 1), low : low + 512]
            if shift:
                part = pltpu.roll(part, shift, 1)
            if s:
                part = jnp.where(lane >= offset_of(s), part[:, :WIDE], part[:, WIDE:])
            else:
                part = part[:, :WIDE]
            start = BLOCK * block + jnp.where(p < 8, 8 * s + p, 16 + 2 * s + p)
            for half in range(2):
                blocks[half, pl.ds(start, 32, stride=128), :] = part[:, 128 * half : 128 * (half + 1)]

    @pl.when(p == LOCAL - 1)
    def _():
        @pl.loop(0, DEVICES)
        def _(d):
            x_hi, core, z, y, x_lo = d // 64, (d // 32) % 2, (d // 8) % 4, (d // 2) % 4, d % 2
            to = z * 32 + y * 8 + x_hi * 4 + x_lo * 2 + core
            rows = pl.ds(pl.multiple_of(d * BLOCK, BLOCK), BLOCK)
            for half in range(2):
                out_ref[to, :, 128 * half : 128 * (half + 1)] = blocks[half, rows, :].astype(BF16)


def dress(vv_vectors, oo_vectors, amps_all):
    return pl.pallas_call(
        dress_kernel,
        grid=(LOCAL,),
        out_shape=jax.ShapeDtypeStruct((DEVICES, BLOCK, WIDE), BF16),
        in_specs=[
            pl.BlockSpec((1, NV, NV), lambda p: (p, 0, 0)),
            pl.BlockSpec((1, NO, NO), lambda p: (p, 0, 0)),
            pl.BlockSpec((NO, NV), lambda p: (0, 0)),
        ],
        out_specs=pl.BlockSpec((DEVICES, BLOCK, WIDE), lambda p: (0, 0, 0)),
        scratch_shapes=[
            pltpu.VMEM((I_ROWS, NV), BF16),
            pltpu.VMEM((I_ROWS, 1024), F32),
            pltpu.VMEM((2, DEVICES * BLOCK, 128), F32),
        ],
        compiler_params=pltpu.CompilerParams(dimension_semantics=("arbitrary",)),
        cost_estimate=pl.CostEstimate(
            flops=2 * LOCAL * I_ROWS * NV * NV, bytes_accessed=2 * LOCAL * NV * NV, transcendentals=0
        ),
        name="dress",
    )(vv_vectors, oo_vectors, amps_all)


def contract_kernel(blocks_ref, slab_ref, out_ref, dressed, slab, tail, slab_tail):
    GROUP = 16
    m = pl.program_id(0)

    @pl.when(m == 0)
    def _():
        lane = lax.broadcasted_iota(jnp.int32, (GROUP * 8, WIDE), 1)

        @pl.loop(0, DEVICES // GROUP)
        def _(g):
            group = pl.ds(g * GROUP, GROUP)
            rows = pl.ds(pl.multiple_of(g * GROUP * 8, GROUP * 8), GROUP * 8)
            parts = [
                blocks_ref[group, 8 * s : 8 * s + 8, :].astype(F32).reshape(GROUP * 8, WIDE)
                for s in range(4)
            ]
            dressed[rows, 0:256] = jnp.where(lane < 250, parts[0], parts[1]).astype(BF16)
            dressed[rows, 256:512] = jnp.where(lane < 244, parts[1], parts[2]).astype(BF16)
            dressed[rows, 512:768] = parts[2].astype(BF16)
            for half in range(2):
                tail[half, rows, :] = parts[3][:, 128 * half : 128 * (half + 1)]
            for c in range(8):
                cols = slice(128 * c, 128 * (c + 1))
                slab[rows, cols] = (
                    slab_ref[group, 8 * c : 8 * c + 8, :].astype(F32).reshape(GROUP * 8, 128).astype(BF16)
                )
            tails = pl.ds(pl.multiple_of(g * GROUP * 16, GROUP * 16), GROUP * 16)
            slab_tail[tails, :] = slab_ref[group, 64:80, :].astype(F32).reshape(GROUP * 16, 128)

        lanes = lax.broadcasted_iota(jnp.int32, (DEVICES, 128), 1) + 128
        for e in range(2):
            rows = slice(1024 + 128 * e, 1152 + 128 * e)
            for half in range(2):
                parts = [tail[half, pl.ds(2 * s + e, DEVICES, stride=8), :] for s in range(3)]
                if half:
                    first = jnp.where(lanes < 250, parts[0], parts[1])
                    second = jnp.where(lanes < 244, parts[1], parts[2])
                else:
                    first, second = parts[0], parts[1]
                for k, part in enumerate((first, second, parts[2])):
                    at = 256 * k + 128 * half
                    dressed[rows, at : at + 128] = part.astype(BF16)
            for c in range(8):
                slab[rows, 128 * c : 128 * (c + 1)] = slab_tail[
                    pl.ds(8 * e + c, DEVICES, stride=16), :
                ].astype(BF16)

    mine = dressed[:, pl.ds(pl.multiple_of(m * WIDE, WIDE), WIDE)]
    out_ref[...] = lax.dot_general(
        mine, slab[...], (((0,), (0,)), ((), ())), preferred_element_type=F32
    )


def contract(blocks, slabs):
    return pl.pallas_call(
        contract_kernel,
        grid=(3,),
        out_shape=jax.ShapeDtypeStruct((750, SLAB), F32),
        in_specs=[
            pl.BlockSpec((DEVICES, BLOCK, WIDE), lambda m: (0, 0, 0)),
            pl.BlockSpec((DEVICES, 80, 128), lambda m: (0, 0, 0)),
        ],
        out_specs=pl.BlockSpec((WIDE, SLAB), lambda m: (m, 0)),
        scratch_shapes=[
            pltpu.VMEM((1280, 768), BF16),
            pltpu.VMEM((1280, SLAB), BF16),
            pltpu.VMEM((2, 1024, 128), F32),
            pltpu.VMEM((2048, 128), F32),
        ],
        compiler_params=pltpu.CompilerParams(dimension_semantics=("arbitrary",)),
        cost_estimate=pl.CostEstimate(
            flops=2 * 768 * 1280 * SLAB, bytes_accessed=8 * 1024 * 1024, transcendentals=0
        ),
        name="contract",
    )(blocks, slabs)


def slab_rows(ov_slab):
    head = ov_slab[:8].reshape(8, 8, 128).transpose(1, 0, 2).reshape(64, 128)
    return jnp.concatenate([head, ov_slab[8:].reshape(16, 128)], axis=0)


def shards(vv_vectors, oo_vectors, ov_slab, amplitudes):
    slabs = lax.all_gather(slab_rows(ov_slab), RING, axis=0, tiled=False)
    amps_all = lax.all_gather(amplitudes, ("x_hi", "core"), axis=0, tiled=True)
    blocks = dress(vv_vectors, oo_vectors, amps_all)
    blocks = lax.all_to_all(blocks, RING, split_axis=0, concat_axis=0, tiled=True)
    return contract(blocks, slabs)


def solution(mesh):
    split = Mesh(mesh.devices.reshape(2, 2, 4, 4, 2), AXES)
    return jax.shard_map(
        shards,
        mesh=split,
        in_specs=(P(AXES, None, None), P(AXES, None, None), P(AXES, None), P(("x_hi", "core"), None)),
        out_specs=P(AXES, None),
        check_vma=False,
    )
```

time: 198 us -> 105 us (0.53)
  the two profiles are of different devices: /device:TPU:4 before, /device:TPU:1 now
where the time goes in v1:
time: 105 us; the launch traced here: 104 us
  blocking collectives  50.1 us (48%)
  Pallas kernels  29.6 us (28%)
  between operations  13.4 us (13%)
  waiting for transfers between devices  8.42 us (8%)
  local copies, waits for them, and re-layouts  2.23 us (2%)
    all_to_all x1, blocking collectives, shards(): lax.all_to_all(blocks, RING, split_axis=0, concat_axis=0, tiled=True)  41.2 us
    pallas_call x1, Pallas kernels, dress(): pl.pallas_call(dress_kernel, grid=(LOCAL,), out_shape=jax.ShapeDtypeStruc...  22.2 us
    all_gather x1, blocking collectives, shards(): amps_all = lax.all_gather(amplitudes, ('x_hi', 'core'), axis=0, tiled=True)  8.82 us
    all_gather x1, waiting for transfers between devices, shards(): slabs = lax.all_gather(slab_rows(ov_slab), RING, axis=0, tiled=False)  8.4 us
    pallas_call x1, Pallas kernels, contract(): pl.pallas_call(contract_kernel, grid=(3,), out_shape=jax.ShapeDtypeStruct...  7.34 us
  transfers between devices with their start and end apart: 1, of which 1 were waited for; matrix products, arithmetic and copies ran while one was open for 1% of the time, Pallas kernels for 21%

profile of v1, /device:TPU:1, one launch (start us, length us, event | category | flops | bytes accessed | tf_op | source)
XLA Modules:
  0.0 104.3 jit_solution(18198522729766577926)
XLA Ops:
  6.5 0.0 all-gather.4.cloned.1.call-start
  6.5 0.7 slice.7
  7.3 0.7 slice_bitcast_fusion
  8.0 0.6 pad_maximum_fusion
  8.6 0.0 all-gather.4.cloned.1.call-update
  8.6 8.8 %all-gather.1 = bf16[4,25,1000]{2,1,0:T(8,128)(2,1)S(1)} all-gather(bf16[1,25,1000]{2,1,0:T(8,128)(2,1)} %bitcast.9), channel_id=1, replica_groups=mesh['x_hi'=2,'core'=2,'z'=4,'y'=4,'x_lo'=2] {'x_hi','core'}, dimensions={0}, use_global_device_ids=true | all-gather | bytes 250000 | tf_op jit(solution)/shard_map/all_gather | solution.py:184
  17.4 0.8 reshape.14.amps_ref
  18.2 22.2 %dress.1 = bf16[128,32,256]{2,1,0:T(8,128)(2,1)} custom-call(bf16[10,1000,1000]{2,1,0:T(8,128)(2,1)} %vv_ref.1, bf16[10,100,100]{2,1,0:T(8,128)(2,1)} %oo_ref.1, bf16[100,1000]{1,0:T(8,128)(2,1)} %reshape.14.amps_ref), custom_call_target="tpu_custom_call" | custom-call | flops 1920000000 | bytes 20000000 | tf_op jit(solution)/shard_map/dress/pallas_call | solution.py:77
  40.4 41.2 %all_to_all.5.blocks_ref = bf16[128,32,256]{2,1,0:T(8,128)(2,1)} all-to-all(bf16[128,32,256]{2,1,0:T(8,128)(2,1)} %dress.1), channel_id=1, replica_groups=mesh['x_hi'=2,'core'=2,'z'=4,'y'=4,'x_lo'=2] {'z','y','x_hi','x_lo','core'}, dimensions={0} | all-to-all | bytes 4194304 | tf_op jit(solution)/shard_map/all_to_all | solution.py:186
  81.7 8.4 %all-gather.4.cloned.1.call-done = bf16[10240,128]{1,0:T(8,128)(2,1)} async-done(((bf16[80,128]{1,0:T(8,128)(2,1)}), bf16[10240,128]{1,0:T(8,128)(2,1)}) %all-gather.4.cloned.1.call-update) | async-done | bytes 2621456 | tf_op jit(solution)/shard_map/all_gather | solution.py:183
  90.1 7.3 %contract.1 = f32[750,1024]{1,0:T(8,128)} custom-call(bf16[128,32,256]{2,1,0:T(8,128)(2,1)} %all_to_all.5.blocks_ref, bf16[128,80,128]{2,1,0:T(8,128)(2,1)} %bitcast.8), custom_call_target="tpu_custom_call" | custom-call | flops 2013265920 | bytes 8388608 | tf_op jit(solution)/shard_map/contract/pallas_call | solution.py:154
  (1 shorter events, 0.0 us)
Async XLA Ops:
  6.5 83.6 %all-gather.4.cloned.1.call-start = ((), (), s32[]{:S(2)}) async-start(), calls=%async_computation.1 | async-start | bytes 2641920 | tf_op jit(solution)/shard_map/all_gather | solution.py:183
Sparse Core Ops, SparseCore 0:
  10.4 79.5 all-gather.3

commit v2 on v1

v2 whole, which is shorter than its diff:
```python
import jax
import jax.numpy as jnp
from jax import lax
from jax.experimental import pallas as pl
from jax.experimental.pallas import tpu as pltpu
from jax.sharding import Mesh, PartitionSpec as P

NO = 100
NV = 1000
I_ROWS = 96
SLAB = 1024
DEVICES = 128
LOCAL = 10
QUARTER = 250
BLOCK = 32
WIDE = 256
AXES = ("x_hi", "core", "z", "y", "x_lo")
RING = ("z", "y", "x_hi", "x_lo", "core")
F32 = jnp.float32
BF16 = jnp.bfloat16


def offset_of(piece):
    return (QUARTER * piece) % WIDE


def dress_kernel(vv_hbm, oo_hbm, amps_0, amps_1, amps_2, amps_3, out_hbm, vv, oo, quarters, spread, amps, window, holes, wide, blocks, out, vv_sem, in_sem, out_sem):
    small = [
        pltpu.make_async_copy(piece, quarters.at[d], in_sem.at[d])
        for d, piece in enumerate((amps_0, amps_1, amps_2, amps_3))
    ]
    small.append(pltpu.make_async_copy(oo_hbm, oo, in_sem.at[4]))
    large = [pltpu.make_async_copy(vv_hbm.at[p], vv.at[p], vv_sem.at[p]) for p in range(LOCAL)]
    for copy in small + large:
        copy.start()

    row = lax.broadcasted_iota(jnp.int32, (I_ROWS, NO), 0)
    col = lax.broadcasted_iota(jnp.int32, (I_ROWS, NO), 1)
    pick = jnp.where(col == 3 * (row % 32) + row // 32, 1.0, 0.0).astype(BF16)
    wide[:, :, 896:1024] = jnp.zeros((2, I_ROWS, 128), F32)
    for half in range(2):
        for spare in range(2):
            blocks[half, pl.ds(30 + spare, DEVICES, stride=BLOCK), :] = jnp.zeros((DEVICES, 128), F32)
    spread[...] = jnp.zeros_like(spread)
    for copy in small:
        copy.wait()
    for d in range(4):
        spread[32 * d : 32 * d + 25, :] = quarters[d]
    me = lax.axis_index(("x_hi", "core"))
    into, at = (lax.broadcasted_iota(jnp.int32, (NO, 128), axis) for axis in (0, 1))
    place = jnp.where((into == 25 * (me ^ (at // 32)) + at % 32) & (at % 32 < 25), 1.0, 0.0).astype(BF16)
    amps[...] = jnp.dot(place, spread[...], preferred_element_type=F32).astype(BF16)
    window[...] = jnp.dot(pick, amps[...], preferred_element_type=F32).astype(BF16)
    for p in range(LOCAL):
        holes[p] = lax.dot_general(
            pick, oo[p], (((1,), (1,)), ((), ())), preferred_element_type=F32
        ).astype(BF16)

    lane = lax.broadcasted_iota(jnp.int32, (32, WIDE), 1)

    def scatter(p):
        for t in range(3):
            for q in range(4):
                block, s = divmod(4 * t + q, 3)
                low = min(QUARTER * q // 128 * 128, 512)
                shift = (offset_of(s) - (QUARTER * q - low)) % 512
                part = wide[p % 2, 32 * t : 32 * (t + 1), low : low + 512]
                if shift:
                    part = pltpu.roll(part, shift, 1)
                if s:
                    part = jnp.where(lane >= offset_of(s), part[:, :WIDE], part[:, WIDE:])
                else:
                    part = part[:, :WIDE]
                start = BLOCK * block + (8 * s + p if p < 8 else 16 + 2 * s + p)
                for half in range(2):
                    blocks[half, pl.ds(start, 32, stride=128), :] = part[:, 128 * half : 128 * (half + 1)]

    for p in range(LOCAL):
        large[p].wait()
        direct = lax.dot_general(
            window[...], vv[p], (((1,), (1,)), ((), ())), preferred_element_type=F32
        )
        hole = jnp.dot(holes[p], amps[...], preferred_element_type=F32)
        wide[p % 2, :, :NV] = direct - hole
        if p:
            scatter(p - 1)
    scatter(LOCAL - 1)

    sends = []
    for chunk in range(8):
        for to in range(16 * chunk, 16 * (chunk + 1)):
            z, y, x_hi, x_lo, core = to // 32, to // 8 % 4, to // 4 % 2, to // 2 % 2, to % 2
            at = BLOCK * (x_hi * 64 + core * 32 + z * 8 + y * 2 + x_lo)
            for half in range(2):
                out[to, :, 128 * half : 128 * (half + 1)] = blocks[half, at : at + BLOCK, :].astype(BF16)
        piece = pl.ds(16 * chunk, 16)
        sends.append(pltpu.make_async_copy(out.at[piece], out_hbm.at[piece], out_sem.at[chunk]))
        sends[-1].start()
    for copy in sends:
        copy.wait()


def dress(vv_vectors, oo_vectors, quarters):
    anywhere = pl.BlockSpec(memory_space=pl.ANY)
    held = pl.BlockSpec(memory_space=pltpu.HBM)
    return pl.pallas_call(
        dress_kernel,
        out_shape=jax.ShapeDtypeStruct((DEVICES, BLOCK, WIDE), BF16),
        in_specs=[held, held] + [anywhere] * 4,
        out_specs=held,
        scratch_shapes=[
            pltpu.VMEM((LOCAL, NV, NV), BF16),
            pltpu.VMEM((LOCAL, NO, NO), BF16),
            pltpu.VMEM((4, 25, NV), BF16),
            pltpu.VMEM((128, NV), BF16),
            pltpu.VMEM((NO, NV), BF16),
            pltpu.VMEM((I_ROWS, NV), BF16),
            pltpu.VMEM((LOCAL, I_ROWS, NO), BF16),
            pltpu.VMEM((2, I_ROWS, 1024), F32),
            pltpu.VMEM((2, DEVICES * BLOCK, 128), F32),
            pltpu.VMEM((DEVICES, BLOCK, WIDE), BF16),
            pltpu.SemaphoreType.DMA((LOCAL,)),
            pltpu.SemaphoreType.DMA((5,)),
            pltpu.SemaphoreType.DMA((8,)),
        ],
        compiler_params=pltpu.CompilerParams(vmem_limit_bytes=48 * 1024 * 1024),
        cost_estimate=pl.CostEstimate(
            flops=2 * LOCAL * I_ROWS * NV * NV, bytes_accessed=2 * LOCAL * NV * NV, transcendentals=0
        ),
        name="dress",
    )(vv_vectors, oo_vectors, *quarters)


def source(n):
    z, y, x, core = (lax.axis_index(a) for a in ("z", "y", ("x_hi", "x_lo"), "core"))
    to_z, to_y, to_x = n % 4, n // 4 % 4, n // 16 % 4
    from_z, from_y, from_x = (z + 4 - to_z) % 4, (y + 4 - to_y) % 4, (x + 4 - to_x) % 4
    return from_z * 32 + from_y * 8 + from_x * 2 + (core + n // 64) % 2


def assemble_kernel(blocks_ref, out_ref, tail):
    lane = lax.broadcasted_iota(jnp.int32, (16, WIDE), 1)

    @pl.loop(0, DEVICES // 16)
    def _(g):
        for pair in range(8):
            n = g * 16 + 2 * pair
            one, two = source(n), source(n + 1)
            parts = [
                jnp.concatenate(
                    [
                        blocks_ref[one, 8 * s : 8 * s + 8, :].astype(F32),
                        blocks_ref[two, 8 * s : 8 * s + 8, :].astype(F32),
                    ],
                    axis=0,
                )
                for s in range(4)
            ]
            rows = pl.ds(pl.multiple_of(n * 8, 16), 16)
            out_ref[rows, 0:256] = jnp.where(lane < 250, parts[0], parts[1]).astype(BF16)
            out_ref[rows, 256:512] = jnp.where(lane < 244, parts[1], parts[2]).astype(BF16)
            out_ref[rows, 512:768] = parts[2].astype(BF16)
            for half in range(2):
                tail[half, rows, :] = parts[3][:, 128 * half : 128 * (half + 1)]

    lanes = lax.broadcasted_iota(jnp.int32, (DEVICES, 128), 1) + 128
    for e in range(2):
        rows = slice(1024 + 128 * e, 1152 + 128 * e)
        for half in range(2):
            parts = [tail[half, pl.ds(2 * s + e, DEVICES, stride=8), :] for s in range(3)]
            if half:
                first = jnp.where(lanes < 250, parts[0], parts[1])
                second = jnp.where(lanes < 244, parts[1], parts[2])
            else:
                first, second = parts[0], parts[1]
            for k, part in enumerate((first, second, parts[2])):
                at = 256 * k + 128 * half
                out_ref[rows, at : at + 128] = part.astype(BF16)


def assemble(blocks):
    return pl.pallas_call(
        assemble_kernel,
        out_shape=jax.ShapeDtypeStruct((1280, 768), BF16),
        scratch_shapes=[pltpu.VMEM((2, 1024, 128), F32)],
        compiler_params=pltpu.CompilerParams(vmem_limit_bytes=24 * 1024 * 1024),
        cost_estimate=pl.CostEstimate(flops=0, bytes_accessed=4 * 1024 * 1024, transcendentals=0),
        name="assemble",
    )(blocks)


def contract_kernel(dressed_ref, mine_ref, other_ref, out_ref, slab, slab_tail):
    GROUP = 16
    m = pl.program_id(0)

    @pl.when(m == 0)
    def _():
        for which, slab_ref in enumerate((mine_ref, other_ref)):

            @pl.loop(0, 64 // GROUP)
            def _(g):
                group = pl.ds(g * GROUP, GROUP)
                at = (64 * which + g * GROUP) * 8
                rows = pl.ds(pl.multiple_of(at, GROUP * 8), GROUP * 8)
                for c in range(8):
                    cols = slice(128 * c, 128 * (c + 1))
                    slab[rows, cols] = (
                        slab_ref[group, 8 * c : 8 * c + 8, :].astype(F32).reshape(GROUP * 8, 128).astype(BF16)
                    )
                tails = pl.ds(pl.multiple_of(2 * at, GROUP * 16), GROUP * 16)
                slab_tail[tails, :] = slab_ref[group, 64:80, :].astype(F32).reshape(GROUP * 16, 128)

        for e in range(2):
            rows = slice(1024 + 128 * e, 1152 + 128 * e)
            for c in range(8):
                slab[rows, 128 * c : 128 * (c + 1)] = slab_tail[
                    pl.ds(8 * e + c, DEVICES, stride=16), :
                ].astype(BF16)

    out_ref[...] = lax.dot_general(
        dressed_ref[...], slab[...], (((0,), (0,)), ((), ())), preferred_element_type=F32
    )


def contract(dressed, mine, other):
    return pl.pallas_call(
        contract_kernel,
        grid=(3,),
        out_shape=jax.ShapeDtypeStruct((750, SLAB), F32),
        in_specs=[
            pl.BlockSpec((1280, WIDE), lambda m: (0, m)),
            pl.BlockSpec((64, 80, 128), lambda m: (0, 0, 0)),
            pl.BlockSpec((64, 80, 128), lambda m: (0, 0, 0)),
        ],
        out_specs=pl.BlockSpec((WIDE, SLAB), lambda m: (m, 0)),
        scratch_shapes=[pltpu.VMEM((1280, SLAB), BF16), pltpu.VMEM((2048, 128), F32)],
        compiler_params=pltpu.CompilerParams(
            dimension_semantics=("arbitrary",), vmem_limit_bytes=32 * 1024 * 1024
        ),
        cost_estimate=pl.CostEstimate(
            flops=2 * 768 * 1280 * SLAB, bytes_accessed=8 * 1024 * 1024, transcendentals=0
        ),
        name="contract",
    )(dressed, mine, other)


def slab_kernel(slab_ref, out_ref, rows):
    for c in range(8):
        part = slab_ref[:, 128 * c : 128 * (c + 1)].astype(F32)
        rows[8 * c : 8 * c + 8, :] = part[0:8]
        for e in range(2):
            rows[64 + 8 * e + c : 65 + 8 * e + c, :] = part[8 + e : 9 + e]
    out_ref[...] = rows[...].astype(BF16)


def slab_rows(ov_slab):
    return pl.pallas_call(
        slab_kernel,
        out_shape=jax.ShapeDtypeStruct((80, 128), BF16),
        scratch_shapes=[pltpu.VMEM((80, 128), F32)],
        compiler_params=pltpu.CompilerParams(vmem_limit_bytes=4 * 1024 * 1024),
        cost_estimate=pl.CostEstimate(flops=0, bytes_accessed=64 * 1024, transcendentals=0),
        name="slab_rows",
    )(ov_slab)


def round_axis(rows, axis):
    others = [lax.ppermute(rows, axis, [(i, (i + d) % 4) for i in range(4)]) for d in (1, 2, 3)]
    return jnp.concatenate([rows, *others], axis=0)


def shards(vv_vectors, oo_vectors, ov_slab, amplitudes):
    group = ("x_hi", "core")
    quarters = [amplitudes] + [lax.ppermute(amplitudes, group, [(i, i ^ d) for i in range(4)]) for d in (1, 2, 3)]
    rows = round_axis(slab_rows(ov_slab), "z")
    rows, quarters = lax.optimization_barrier((rows, quarters))
    rows = round_axis(rows, "y")
    blocks = dress(vv_vectors, oo_vectors, quarters)
    rows, blocks = lax.optimization_barrier((rows, blocks))
    blocks = lax.all_to_all(blocks, RING, split_axis=0, concat_axis=0, tiled=True)
    rows = round_axis(rows, ("x_hi", "x_lo"))
    other = lax.ppermute(rows, "core", [(0, 1), (1, 0)])
    return contract(assemble(blocks), rows.reshape(64, 80, 128), other.reshape(64, 80, 128))


def solution(mesh):
    split = Mesh(mesh.devices.reshape(2, 2, 4, 4, 2), AXES)
    return jax.shard_map(
        shards,
        mesh=split,
        in_specs=(P(AXES, None, None), P(AXES, None, None), P(AXES, None), P(("x_hi", "core"), None)),
        out_specs=P(AXES, None),
        check_vma=False,
    )
```

time: 105 us -> 90.4 us (0.86)
  blocking collectives: 50.1 us -> 0 us
  starting transfers between devices: 0.01 us -> 30.5 us
  waiting for transfers between devices: 8.42 us -> 28.4 us
  between operations: 13.4 us -> 0.1 us
  Pallas kernels: 29.6 us -> 23.7 us
  local copies, waits for them, and re-layouts: 2.23 us -> 6.59 us
    all_to_all x1 -> x0, blocking collectives: 41.2 us -> none  [shards(): lax.all_to_all(blocks, RING, split_axis=0, concat_axis=0, tiled=True)]
    ppermute x0 -> x13, starting transfers between devices: none -> 21.3 us  [the longest x9 11.8 us: round_axis(): lax.ppermute(rows, axis, [(i, (i + d) % 4) for i in range(4)])]
    all_to_all x0 -> x1, waiting for transfers between devices: none -> 20.6 us  [shards(): lax.all_to_all(blocks, RING, split_axis=0, concat_axis=0, tiled=True)]
    all_to_all x0 -> x1, starting transfers between devices: none -> 9.19 us  [shards(): lax.all_to_all(blocks, RING, split_axis=0, concat_axis=0, tiled=True)]
    all_gather x1 -> x0, blocking collectives: 8.82 us -> none  [shards(): amps_all = lax.all_gather(amplitudes, ('x_hi', 'core'), axis=0, tiled=True)]
    all_gather x1 -> x0, waiting for transfers between devices: 8.4 us -> none  [shards(): slabs = lax.all_gather(slab_rows(ov_slab), RING, axis=0, tiled=False)]
    ppermute x0 -> x13, waiting for transfers between devices: none -> 7.78 us  [the longest x3 5.29 us: shards(): lax.ppermute(amplitudes, group, [(i, i ^ d) for i in range(4)])]
    unnamed x1 -> x9, local copies, waits for them, and re-layouts: 0.78 us -> 5.57 us
  transfers between devices with their start and end apart: 1 -> 14, of which waited for: 1 -> 5; matrix products, arithmetic and copies ran while one was open for 1% -> 5% of each run, Pallas kernels for 21% -> 20%
where the time goes in v2:
time: 90.4 us; the launch traced here: 90 us
  starting transfers between devices  30.5 us (34%)
  waiting for transfers between devices  28.4 us (31%)
  Pallas kernels  23.7 us (26%)
  local copies, waits for them, and re-layouts  6.59 us (7%)
    all_to_all x1, waiting for transfers between devices, shards(): lax.all_to_all(blocks, RING, split_axis=0, concat_axis=0, tiled=True)  20.6 us
    pallas_call x1, Pallas kernels, dress(): pl.pallas_call(dress_kernel, out_shape=jax.ShapeDtypeStruct((DEVICES, BLO...  13.6 us
    ppermute x9, starting transfers between devices, round_axis(): lax.ppermute(rows, axis, [(i, (i + d) % 4) for i in range(4)])  11.8 us
    all_to_all x1, starting transfers between devices, shards(): lax.all_to_all(blocks, RING, split_axis=0, concat_axis=0, tiled=True)  9.19 us
    pallas_call x1, Pallas kernels, contract(): pl.pallas_call(contract_kernel, grid=(3,), out_shape=jax.ShapeDtypeStruct...  6.04 us
    unnamed x9, local copies, waits for them, and re-layouts  5.57 us
    ppermute x3, waiting for transfers between devices, shards(): lax.ppermute(amplitudes, group, [(i, i ^ d) for i in range(4)])  5.29 us
    ppermute x1, starting transfers between devices, shards(): other = lax.ppermute(rows, 'core', [(0, 1), (1, 0)])  4.82 us
  transfers between devices with their start and end apart: 14, of which 5 were waited for; matrix products, arithmetic and copies ran while one was open for 5% of the time, Pallas kernels for 20%

profile of v2, /device:TPU:1, one launch (start us, length us, event | category | flops | bytes accessed | tf_op | source)
XLA Modules:
  0.0 90.0 jit_solution(2968482704062807515)
XLA Ops:
  0.0 0.0 copy-start.2
  0.0 0.8 copy-done.2
  0.8 4.6 %collective-permute-start.2 = (bf16[80,128]{1,0:T(8,128)(2,1)S(1)}, bf16[80,128]{1,0:T(8,128)(2,1)S(1)}, u32[]{:S(2)}, u32[]{:S(2)}) collective-permute-start(bf16[80,128]{1,0:T(8,128)(2,1)S(1)} %slab_rows.1), channel_id=1, source_target_pairs={{0,24},{8,0},{16,8},{24,16},{1,25},{9,1},{17,9},{25,17},{2,26},{10... | collective-permute-start | bytes 61448 | tf_op jit(solution)/shard_map/ppermute | solution.py:268
  5.4 0.0 collective-permute-start.1
  5.4 0.7 collective-permute-start
  6.1 2.7 %collective-permute-start.4 = (bf16[25,1000]{1,0:T(8,128)(2,1)}, bf16[25,1000]{1,0:T(8,128)(2,1)S(1)}, u32[]{:S(2)}, u32[]{:S(2)}) collective-permute-start(bf16[25,1000]{1,0:T(8,128)(2,1)} %amps_0), channel_id=1, source_target_pairs={{0,64},{32,96},{64,0},{96,32},{1,65},{33,97},{65,1},{97,33},{2,66}... | collective-permute-start | bytes 150008 | tf_op jit(solution)/shard_map/ppermute | solution.py:274
  8.9 1.8 %collective-permute-start.3 = (bf16[25,1000]{1,0:T(8,128)(2,1)}, bf16[25,1000]{1,0:T(8,128)(2,1)S(1)}, u32[]{:S(2)}, u32[]{:S(2)}) collective-permute-start(bf16[25,1000]{1,0:T(8,128)(2,1)} %amps_0), channel_id=1, source_target_pairs={{0,32},{32,0},{64,96},{96,64},{1,33},{33,1},{65,97},{97,65},{2,34}... | collective-permute-start | bytes 150008 | tf_op jit(solution)/shard_map/ppermute | solution.py:274
  10.7 0.0 collective-permute-done.2
  10.7 0.1 collective-permute-start.5
  10.8 0.0 collective-permute-done.1
  10.8 0.0 collective-permute-done
  10.8 0.5 collective-permute-done.4.amps_2
  11.2 0.5 collective-permute-done.3.amps_1
  11.8 4.3 %collective-permute-done.5.amps_3 = bf16[25,1000]{1,0:T(8,128)(2,1)S(1)} collective-permute-done((bf16[25,1000]{1,0:T(8,128)(2,1)}, bf16[25,1000]{1,0:T(8,128)(2,1)S(1)}, u32[]{:S(2)}, u32[]{:S(2)}) %collective-permute-start.5) | collective-permute-done | bytes 50032 | tf_op jit(solution)/shard_map/ppermute | solution.py:274
  16.1 2.7 %collective-permute-start.8 = (bf16[320,128]{1,0:T(8,128)(2,1)S(1)}, bf16[320,128]{1,0:T(8,128)(2,1)S(1)}, u32[]{:S(2)}, u32[]{:S(2)}) collective-permute-start(bf16[320,128]{1,0:T(8,128)(2,1)S(1)} %pad_maximum_fusion.1), channel_id=1, source_target_pairs={{0,6},{2,0},{4,2},{6,4},{1,7},{3,1},{5,3},{7,5},{8,14},{10,8},{12,... | collective-permute-start | bytes 245768 | tf_op jit(solution)/shard_map/ppermute | solution.py:268
  18.8 0.3 collective-permute-start.7
  19.2 0.7 collective-permute-start.6
  19.9 0.0 copy-start
  19.9 0.9 %copy-done = bf16[10,100,100]{2,1,0:T(8,128)(2,1)S(1)} copy-done((bf16[10,100,100]{2,1,0:T(8,128)(2,1)S(1)}, bf16[10,100,100]{2,1,0:T(8,128)(2,1)}, u32[]{:S(2)}) %copy-start) | copy-done | bytes 200024
  20.8 0.0 copy-start.1
  20.8 0.8 copy-done.1
  21.7 13.6 %dress.1 = bf16[128,32,256]{2,1,0:T(8,128)(2,1)} custom-call(bf16[10,1000,1000]{2,1,0:T(8,128)(2,1)} %vv_hbm.1, bf16[10,100,100]{2,1,0:T(8,128)(2,1)S(1)} %copy-done, bf16[25,1000]{1,0:T(8,128)(2,1)S(1)} %copy-done.1, bf16[25,1000]{1,0:T(8,128)(2,1)S(1)} %collective-permute-done.3.amps_1, bf16[25,1000]{1,0:T(8,128)(2,1)S(1)} %collective-permute-done.4.amps_2, ...), custom_call_target="tpu_custom_call" | custom-call | flops 1920000000 | bytes 20000000 | tf_op jit(solution)/shard_map/dress/pallas_call | solution.py:106
  35.2 0.0 collective-permute-done.8
  35.2 0.0 collective-permute-done.7
  35.2 0.0 collective-permute-done.6
  35.3 0.7 pad_maximum_fusion
  36.0 0.3 collective-permute-start.9
  36.3 2.4 %collective-permute-start.11 = (bf16[1280,128]{1,0:T(8,128)(2,1)}, bf16[1280,128]{1,0:T(8,128)(2,1)}, u32[]{:S(2)}, u32[]{:S(2)}) collective-permute-start(bf16[1280,128]{1,0:T(8,128)(2,1)} %pad_maximum_fusion), channel_id=1, source_target_pairs={{0,65},{1,0},{64,1},{65,64},{2,67},{3,2},{66,3},{67,66},{4,69},{5,... | collective-permute-start | bytes 983048 | tf_op jit(solution)/shard_map/ppermute | solution.py:268
  38.7 0.0 collective-permute-start.10
  38.7 9.2 %all-to-all-start = ((bf16[128,32,256]{2,1,0:T(8,128)(2,1)}), bf16[128,32,256]{2,1,0:T(8,128)(2,1)S(1)}, u32[]{:S(2)}, u32[]{:S(2)}) async-start(bf16[128,32,256]{2,1,0:T(8,128)(2,1)} %dress.1), calls=%async_computation | async-start | bytes 4194304 | tf_op jit(solution)/shard_map/all_to_all | solution.py:280
  47.9 1.0 %constant_dynamic-update-slice_fusion.3 = bf16[5120,128]{1,0:T(8,128)(2,1)S(1)} fusion(bf16[1280,128]{1,0:T(8,128)(2,1)} %pad_maximum_fusion), kind=kLoop, calls=%fused_computation.5 | loop fusion | bytes 655360
  48.9 0.0 collective-permute-done.9
  48.9 1.0 %constant_dynamic-update-slice_fusion.2 = bf16[5120,128]{1,0:T(8,128)(2,1)S(1)} fusion(bf16[5120,128]{1,0:T(8,128)(2,1)S(1)} %constant_dynamic-update-slice_fusion.3, bf16[1280,128]{1,0:T(8,128)(2,1)} %collective-permute-done.9), kind=kLoop, calls=%fused_computation.4 | loop fusion | bytes 655360
  49.9 2.5 %collective-permute-done.10 = bf16[1280,128]{1,0:T(8,128)(2,1)} collective-permute-done((bf16[1280,128]{1,0:T(8,128)(2,1)}, bf16[1280,128]{1,0:T(8,128)(2,1)}, u32[]{:S(2)}, u32[]{:S(2)}) %collective-permute-start.10) | collective-permute-done | bytes 327712 | tf_op jit(solution)/shard_map/ppermute | solution.py:268
  52.4 1.0 %constant_dynamic-update-slice_fusion.1 = bf16[5120,128]{1,0:T(8,128)(2,1)S(1)} fusion(bf16[5120,128]{1,0:T(8,128)(2,1)S(1)} %constant_dynamic-update-slice_fusion.2, bf16[1280,128]{1,0:T(8,128)(2,1)} %collective-permute-done.10), kind=kLoop, calls=%fused_computation.3 | loop fusion | bytes 655360
  53.4 0.0 collective-permute-done.11
  53.4 1.0 %constant_dynamic-update-slice_fusion = bf16[5120,128]{1,0:T(8,128)(2,1)S(1)} fusion(bf16[5120,128]{1,0:T(8,128)(2,1)S(1)} %constant_dynamic-update-slice_fusion.1, bf16[1280,128]{1,0:T(8,128)(2,1)} %collective-permute-done.11), kind=kLoop, calls=%fused_computation.2 | loop fusion | bytes 655360 | tf_op jit(solution)/shard_map/concatenate | solution.py:269
  54.4 4.8 %collective-permute-start.12 = (bf16[5120,128]{1,0:T(8,128)(2,1)S(1)}, bf16[5120,128]{1,0:T(8,128)(2,1)}, u32[]{:S(2)}, u32[]{:S(2)}) collective-permute-start(bf16[5120,128]{1,0:T(8,128)(2,1)S(1)} %constant_dynamic-update-slice_fusion), channel_id=1, source_target_pairs={{0,32},{32,0},{1,33},{33,1},{2,34},{34,2},{3,35},{35,3},{4,36},{36... | collective-permute-start | bytes 3932168 | tf_op jit(solution)/shard_map/ppermute | solution.py:282
  59.3 20.6 %all-to-all-done.blocks_ref = bf16[128,32,256]{2,1,0:T(8,128)(2,1)S(1)} async-done(((bf16[128,32,256]{2,1,0:T(8,128)(2,1)}), bf16[128,32,256]{2,1,0:T(8,128)(2,1)S(1)}, u32[]{:S(2)}, u32[]{:S(2)}) %all-to-all-start) | async-done | bytes 2097184 | tf_op jit(solution)/shard_map/all_to_all | solution.py:280
  79.8 4.1 %assemble.1.dressed_ref = bf16[1280,768]{1,0:T(8,128)(2,1)S(1)} custom-call(bf16[128,32,256]{2,1,0:T(8,128)(2,1)S(1)} %all-to-all-done.blocks_ref), custom_call_target="tpu_custom_call" | custom-call | bytes 4194304 | tf_op jit(solution)/shard_map/assemble/pallas_call | solution.py:182
  83.9 0.0 collective-permute-done.12
  83.9 6.0 %contract.1 = f32[750,1024]{1,0:T(8,128)} custom-call(bf16[1280,768]{1,0:T(8,128)(2,1)S(1)} %assemble.1.dressed_ref, bf16[64,80,128]{2,1,0:T(8,128)(2,1)S(1)} %bitcast.2, bf16[64,80,128]{2,1,0:T(8,128)(2,1)} %bitcast.1.other_ref), custom_call_target="tpu_custom_call" | custom-call | flops 2013265920 | bytes 8388608 | tf_op jit(solution)/shard_map/contract/pallas_call | solution.py:226
  (2 shorter events, 0.0 us)
Async XLA Ops:
  0.0 0.8 copy-start.2
  0.8 9.9 %collective-permute-start.2 = (bf16[80,128]{1,0:T(8,128)(2,1)S(1)}, bf16[80,128]{1,0:T(8,128)(2,1)S(1)}, u32[]{:S(2)}, u32[]{:S(2)}) collective-permute-start(bf16[80,128]{1,0:T(8,128)(2,1)S(1)} %slab_rows.1), channel_id=1, source_target_pairs={{0,24},{8,0},{16,8},{24,16},{1,25},{9,1},{17,9},{25,17},{2,26},{10... | collective-permute-start | bytes 61448 | tf_op jit(solution)/shard_map/ppermute | solution.py:268
  5.4 5.4 %collective-permute-start.1 = (bf16[80,128]{1,0:T(8,128)(2,1)S(1)}, bf16[80,128]{1,0:T(8,128)(2,1)S(1)}, u32[]{:S(2)}, u32[]{:S(2)}) collective-permute-start(bf16[80,128]{1,0:T(8,128)(2,1)S(1)} %slab_rows.1), channel_id=1, source_target_pairs={{0,16},{8,24},{16,0},{24,8},{1,17},{9,25},{17,1},{25,9},{2,18},{10... | collective-permute-start | bytes 61448 | tf_op jit(solution)/shard_map/ppermute | solution.py:268
  5.4 5.4 %collective-permute-start = (bf16[80,128]{1,0:T(8,128)(2,1)S(1)}, bf16[80,128]{1,0:T(8,128)(2,1)S(1)}, u32[]{:S(2)}, u32[]{:S(2)}) collective-permute-start(bf16[80,128]{1,0:T(8,128)(2,1)S(1)} %slab_rows.1), channel_id=1, source_target_pairs={{0,8},{8,16},{16,24},{24,0},{1,9},{9,17},{17,25},{25,1},{2,10},{10... | collective-permute-start | bytes 61448 | tf_op jit(solution)/shard_map/ppermute | solution.py:268
  6.1 5.1 %collective-permute-start.4 = (bf16[25,1000]{1,0:T(8,128)(2,1)}, bf16[25,1000]{1,0:T(8,128)(2,1)S(1)}, u32[]{:S(2)}, u32[]{:S(2)}) collective-permute-start(bf16[25,1000]{1,0:T(8,128)(2,1)} %amps_0), channel_id=1, source_target_pairs={{0,64},{32,96},{64,0},{96,32},{1,65},{33,97},{65,1},{97,33},{2,66}... | collective-permute-start | bytes 150008 | tf_op jit(solution)/shard_map/ppermute | solution.py:274
  8.9 2.9 %collective-permute-start.3 = (bf16[25,1000]{1,0:T(8,128)(2,1)}, bf16[25,1000]{1,0:T(8,128)(2,1)S(1)}, u32[]{:S(2)}, u32[]{:S(2)}) collective-permute-start(bf16[25,1000]{1,0:T(8,128)(2,1)} %amps_0), channel_id=1, source_target_pairs={{0,32},{32,0},{64,96},{96,64},{1,33},{33,1},{65,97},{97,65},{2,34}... | collective-permute-start | bytes 150008 | tf_op jit(solution)/shard_map/ppermute | solution.py:274
  10.7 5.4 %collective-permute-start.5 = (bf16[25,1000]{1,0:T(8,128)(2,1)}, bf16[25,1000]{1,0:T(8,128)(2,1)S(1)}, u32[]{:S(2)}, u32[]{:S(2)}) collective-permute-start(bf16[25,1000]{1,0:T(8,128)(2,1)} %amps_0), channel_id=1, source_target_pairs={{0,96},{32,64},{64,32},{96,0},{1,97},{33,65},{65,33},{97,1},{2,98}... | collective-permute-start | bytes 150008 | tf_op jit(solution)/shard_map/ppermute | solution.py:274
  16.1 19.1 %collective-permute-start.8 = (bf16[320,128]{1,0:T(8,128)(2,1)S(1)}, bf16[320,128]{1,0:T(8,128)(2,1)S(1)}, u32[]{:S(2)}, u32[]{:S(2)}) collective-permute-start(bf16[320,128]{1,0:T(8,128)(2,1)S(1)} %pad_maximum_fusion.1), channel_id=1, source_target_pairs={{0,6},{2,0},{4,2},{6,4},{1,7},{3,1},{5,3},{7,5},{8,14},{10,8},{12,... | collective-permute-start | bytes 245768 | tf_op jit(solution)/shard_map/ppermute | solution.py:268
  18.8 16.4 %collective-permute-start.7 = (bf16[320,128]{1,0:T(8,128)(2,1)S(1)}, bf16[320,128]{1,0:T(8,128)(2,1)S(1)}, u32[]{:S(2)}, u32[]{:S(2)}) collective-permute-start(bf16[320,128]{1,0:T(8,128)(2,1)S(1)} %pad_maximum_fusion.1), channel_id=1, source_target_pairs={{0,4},{2,6},{4,0},{6,2},{1,5},{3,7},{5,1},{7,3},{8,12},{10,14},{12... | collective-permute-start | bytes 245768 | tf_op jit(solution)/shard_map/ppermute | solution.py:268
  19.2 16.1 %collective-permute-start.6 = (bf16[320,128]{1,0:T(8,128)(2,1)S(1)}, bf16[320,128]{1,0:T(8,128)(2,1)S(1)}, u32[]{:S(2)}, u32[]{:S(2)}) collective-permute-start(bf16[320,128]{1,0:T(8,128)(2,1)S(1)} %pad_maximum_fusion.1), channel_id=1, source_target_pairs={{0,2},{2,4},{4,6},{6,0},{1,3},{3,5},{5,7},{7,1},{8,10},{10,12},{12... | collective-permute-start | bytes 245768 | tf_op jit(solution)/shard_map/ppermute | solution.py:268
  19.9 1.0 %copy-start = (bf16[10,100,100]{2,1,0:T(8,128)(2,1)S(1)}, bf16[10,100,100]{2,1,0:T(8,128)(2,1)}, u32[]{:S(2)}) copy-start(bf16[10,100,100]{2,1,0:T(8,128)(2,1)} %oo_hbm.1) | copy-start | bytes 600004
  20.8 0.8 copy-start.1
  36.0 12.9 %collective-permute-start.9 = (bf16[1280,128]{1,0:T(8,128)(2,1)}, bf16[1280,128]{1,0:T(8,128)(2,1)}, u32[]{:S(2)}, u32[]{:S(2)}) collective-permute-start(bf16[1280,128]{1,0:T(8,128)(2,1)} %pad_maximum_fusion), channel_id=1, source_target_pairs={{0,1},{1,64},{64,65},{65,0},{2,3},{3,66},{66,67},{67,2},{4,5},{5,6... | collective-permute-start | bytes 983048 | tf_op jit(solution)/shard_map/ppermute | solution.py:268
  36.3 17.1 %collective-permute-start.11 = (bf16[1280,128]{1,0:T(8,128)(2,1)}, bf16[1280,128]{1,0:T(8,128)(2,1)}, u32[]{:S(2)}, u32[]{:S(2)}) collective-permute-start(bf16[1280,128]{1,0:T(8,128)(2,1)} %pad_maximum_fusion), channel_id=1, source_target_pairs={{0,65},{1,0},{64,1},{65,64},{2,67},{3,2},{66,3},{67,66},{4,69},{5,... | collective-permute-start | bytes 983048 | tf_op jit(solution)/shard_map/ppermute | solution.py:268
  38.7 13.7 %collective-permute-start.10 = (bf16[1280,128]{1,0:T(8,128)(2,1)}, bf16[1280,128]{1,0:T(8,128)(2,1)}, u32[]{:S(2)}, u32[]{:S(2)}) collective-permute-start(bf16[1280,128]{1,0:T(8,128)(2,1)} %pad_maximum_fusion), channel_id=1, source_target_pairs={{0,64},{1,65},{64,0},{65,1},{2,66},{3,67},{66,2},{67,3},{4,68},{5,... | collective-permute-start | bytes 983048 | tf_op jit(solution)/shard_map/ppermute | solution.py:268
  38.7 41.2 %all-to-all-start = ((bf16[128,32,256]{2,1,0:T(8,128)(2,1)}), bf16[128,32,256]{2,1,0:T(8,128)(2,1)S(1)}, u32[]{:S(2)}, u32[]{:S(2)}) async-start(bf16[128,32,256]{2,1,0:T(8,128)(2,1)} %dress.1), calls=%async_computation | async-start | bytes 4194304 | tf_op jit(solution)/shard_map/all_to_all | solution.py:280
  54.4 29.5 %collective-permute-start.12 = (bf16[5120,128]{1,0:T(8,128)(2,1)S(1)}, bf16[5120,128]{1,0:T(8,128)(2,1)}, u32[]{:S(2)}, u32[]{:S(2)}) collective-permute-start(bf16[5120,128]{1,0:T(8,128)(2,1)S(1)} %constant_dynamic-update-slice_fusion), channel_id=1, source_target_pairs={{0,32},{32,0},{1,33},{33,1},{2,34},{34,2},{3,35},{35,3},{4,36},{36... | collective-permute-start | bytes 3932168 | tf_op jit(solution)/shard_map/ppermute | solution.py:282

commit v3 on v2

v3 whole, which is shorter than its diff:
```python
import jax
import jax.numpy as jnp
from jax import lax
from jax.experimental import pallas as pl
from jax.experimental.pallas import tpu as pltpu
from jax.sharding import Mesh, PartitionSpec as P

NO = 100
NV = 1000
I_ROWS = 96
SLAB = 1024
DEVICES = 128
LOCAL = 10
QUARTER = 250
DRESS_VMEM = 48 * 1024 * 1024
BLOCK = 32
WIDE = 256
AXES = ("x_hi", "core", "z", "y", "x_lo")
RING = ("z", "y", "x_hi", "x_lo", "core")
F32 = jnp.float32
BF16 = jnp.bfloat16


def offset_of(piece):
    return (QUARTER * piece) % WIDE


def picked_rows():
    row = lax.broadcasted_iota(jnp.int32, (I_ROWS, NO), 0)
    col = lax.broadcasted_iota(jnp.int32, (I_ROWS, NO), 1)
    return jnp.where(col == 3 * (row % 32) + row // 32, 1.0, 0.0).astype(BF16)


def holes_kernel(oo_ref, out_ref):
    pick = picked_rows()
    for p in range(LOCAL):
        out_ref[p] = lax.dot_general(
            pick, oo_ref[p], (((1,), (1,)), ((), ())), preferred_element_type=F32
        ).astype(BF16)


def hole_factors(oo_vectors):
    return pl.pallas_call(
        holes_kernel,
        out_shape=jax.ShapeDtypeStruct((LOCAL, I_ROWS, NO), BF16),
        compiler_params=pltpu.CompilerParams(vmem_limit_bytes=4 * 1024 * 1024),
        cost_estimate=pl.CostEstimate(flops=2 * LOCAL * NO**3, bytes_accessed=512 * 1024, transcendentals=0),
        name="hole_factors",
    )(oo_vectors)


def dress_kernel(vv_hbm, holes_hbm, amps_0, amps_1, amps_2, amps_3, out_hbm, vv, holes, quarters, spread, amps, window, wide, blocks, out, vv_sem, in_sem, out_sem):
    small = [
        pltpu.make_async_copy(piece, quarters.at[d], in_sem.at[d])
        for d, piece in enumerate((amps_0, amps_1, amps_2, amps_3))
    ]
    small.append(pltpu.make_async_copy(holes_hbm, holes, in_sem.at[4]))
    large = [pltpu.make_async_copy(vv_hbm.at[p], vv.at[p], vv_sem.at[p]) for p in range(LOCAL)]
    for copy in small + large:
        copy.start()

    pick = picked_rows()
    wide[:, :, 896:1024] = jnp.zeros((2, I_ROWS, 128), F32)
    for half in range(2):
        for spare in range(2):
            blocks[half, pl.ds(30 + spare, DEVICES, stride=BLOCK), :] = jnp.zeros((DEVICES, 128), F32)
    spread[...] = jnp.zeros_like(spread)
    for copy in small:
        copy.wait()
    for d in range(4):
        spread[32 * d : 32 * d + 25, :] = quarters[d]
    me = lax.axis_index(("x_hi", "core"))
    into, at = (lax.broadcasted_iota(jnp.int32, (NO, 128), axis) for axis in (0, 1))
    place = jnp.where((into == 25 * (me ^ (at // 32)) + at % 32) & (at % 32 < 25), 1.0, 0.0).astype(BF16)
    amps[...] = jnp.dot(place, spread[...], preferred_element_type=F32).astype(BF16)
    window[...] = jnp.dot(pick, amps[...], preferred_element_type=F32).astype(BF16)

    lane = lax.broadcasted_iota(jnp.int32, (32, WIDE), 1)

    def scatter(p):
        for t in range(3):
            for q in range(4):
                block, s = divmod(4 * t + q, 3)
                low = min(QUARTER * q // 128 * 128, 512)
                shift = (offset_of(s) - (QUARTER * q - low)) % 512
                part = wide[p % 2, 32 * t : 32 * (t + 1), low : low + 512]
                if shift:
                    part = pltpu.roll(part, shift, 1)
                if s:
                    part = jnp.where(lane >= offset_of(s), part[:, :WIDE], part[:, WIDE:])
                else:
                    part = part[:, :WIDE]
                start = BLOCK * block + (8 * s + p if p < 8 else 16 + 2 * s + p)
                for half in range(2):
                    blocks[half, pl.ds(start, 32, stride=128), :] = part[:, 128 * half : 128 * (half + 1)]

    for p in range(LOCAL):
        large[p].wait()
        direct = lax.dot_general(
            window[...], vv[p], (((1,), (1,)), ((), ())), preferred_element_type=F32
        )
        hole = jnp.dot(holes[p], amps[...], preferred_element_type=F32)
        wide[p % 2, :, :NV] = direct - hole
        if p:
            scatter(p - 1)
    scatter(LOCAL - 1)

    sends = []
    for chunk in range(8):
        for to in range(16 * chunk, 16 * (chunk + 1)):
            z, y, x_hi, x_lo, core = to // 32, to // 8 % 4, to // 4 % 2, to // 2 % 2, to % 2
            at = BLOCK * (x_hi * 64 + core * 32 + z * 8 + y * 2 + x_lo)
            for half in range(2):
                out[to, :, 128 * half : 128 * (half + 1)] = blocks[half, at : at + BLOCK, :].astype(BF16)
        piece = pl.ds(16 * chunk, 16)
        sends.append(pltpu.make_async_copy(out.at[piece], out_hbm.at[piece], out_sem.at[chunk]))
        sends[-1].start()
    for copy in sends:
        copy.wait()


def dress(vv_vectors, holes, quarters):
    anywhere = pl.BlockSpec(memory_space=pl.ANY)
    held = pl.BlockSpec(memory_space=pltpu.HBM)
    return pl.pallas_call(
        dress_kernel,
        out_shape=jax.ShapeDtypeStruct((DEVICES, BLOCK, WIDE), BF16),
        in_specs=[held, held] + [anywhere] * 4,
        out_specs=held,
        scratch_shapes=[
            pltpu.VMEM((LOCAL, NV, NV), BF16),
            pltpu.VMEM((LOCAL, I_ROWS, NO), BF16),
            pltpu.VMEM((4, 25, NV), BF16),
            pltpu.VMEM((128, NV), BF16),
            pltpu.VMEM((NO, NV), BF16),
            pltpu.VMEM((I_ROWS, NV), BF16),
            pltpu.VMEM((2, I_ROWS, 1024), F32),
            pltpu.VMEM((2, DEVICES * BLOCK, 128), F32),
            pltpu.VMEM((DEVICES, BLOCK, WIDE), BF16),
            pltpu.SemaphoreType.DMA((LOCAL,)),
            pltpu.SemaphoreType.DMA((5,)),
            pltpu.SemaphoreType.DMA((8,)),
        ],
        compiler_params=pltpu.CompilerParams(vmem_limit_bytes=DRESS_VMEM),
        cost_estimate=pl.CostEstimate(
            flops=2 * LOCAL * I_ROWS * NV * NV, bytes_accessed=2 * LOCAL * NV * NV, transcendentals=0
        ),
        name="dress",
    )(vv_vectors, holes, *quarters)


def order_kernel(mine_ref, other_ref, out_ref, tail):
    me_z, me_y, me_x, me_core = (lax.axis_index(a) for a in ("z", "y", ("x_hi", "x_lo"), "core"))

    @pl.loop(0, DEVICES // 2)
    def _(chip):
        z, y, x = chip // 16, chip // 4 % 4, chip % 4
        at = (me_x + 4 - x) % 4 * 16 + (me_y + 4 - y) % 4 * 4 + (me_z + 4 - z) % 4
        mine, other = mine_ref[at].astype(F32), other_ref[at].astype(F32)
        one, two = jnp.where(me_core == 0, mine, other), jnp.where(me_core == 0, other, mine)
        rows = pl.ds(pl.multiple_of(chip * 16, 16), 16)
        for c in range(8):
            both = jnp.concatenate([one[8 * c : 8 * c + 8], two[8 * c : 8 * c + 8]], axis=0)
            out_ref[rows, 128 * c : 128 * (c + 1)] = both.astype(BF16)
        start = pl.multiple_of(chip * 32, 32)
        tail[pl.ds(start, 16), :] = one[64:80]
        tail[pl.ds(start + 16, 16), :] = two[64:80]

    for e in range(2):
        for c in range(8):
            out_ref[1024 + 128 * e : 1152 + 128 * e, 128 * c : 128 * (c + 1)] = tail[
                pl.ds(8 * e + c, DEVICES, stride=16), :
            ].astype(BF16)


def ordered(mine, other):
    return pl.pallas_call(
        order_kernel,
        out_shape=jax.ShapeDtypeStruct((1280, SLAB), BF16),
        scratch_shapes=[pltpu.VMEM((2048, 128), F32)],
        compiler_params=pltpu.CompilerParams(vmem_limit_bytes=16 * 1024 * 1024),
        cost_estimate=pl.CostEstimate(flops=0, bytes_accessed=6 * 1024 * 1024, transcendentals=0),
        name="ordered",
    )(mine, other)


def contract_kernel(blocks_ref, slab_ref, out_ref, dressed, tail):
    GROUP = 16
    m = pl.program_id(0)
    after = jnp.minimum(m + 1, 2)
    limit = jnp.where(m < 2, 250 - 6 * m, WIDE)

    @pl.when(m == 0)
    def _():
        @pl.loop(0, DEVICES // GROUP, unroll=2)
        def _(g):
            group = pl.ds(g * GROUP, GROUP)
            rows = pl.ds(pl.multiple_of(g * GROUP * 8, GROUP * 8), GROUP * 8)
            for half in range(2):
                part = blocks_ref[group, 24:32, 128 * half : 128 * (half + 1)]
                tail[half, rows, :] = part.astype(F32).reshape(GROUP * 8, 128)

    lane = lax.broadcasted_iota(jnp.int32, (GROUP * 8, WIDE), 1)

    @pl.loop(0, DEVICES // GROUP, unroll=2)
    def _(g):
        group = pl.ds(g * GROUP, GROUP)
        rows = pl.ds(pl.multiple_of(g * GROUP * 8, GROUP * 8), GROUP * 8)
        one, two = (
            blocks_ref[group, pl.ds(pl.multiple_of(8 * s, 8), 8), :].astype(F32).reshape(GROUP * 8, WIDE)
            for s in (m, after)
        )
        dressed[rows, :] = jnp.where(lane < limit, one, two).astype(BF16)

    lanes = lax.broadcasted_iota(jnp.int32, (DEVICES, 128), 1)
    for e in range(2):
        rows = slice(1024 + 128 * e, 1152 + 128 * e)
        for half in range(2):
            one, two = (tail[half, pl.ds(2 * s + e, DEVICES, stride=8), :] for s in (m, after))
            dressed[rows, 128 * half : 128 * (half + 1)] = jnp.where(
                lanes + 128 * half < limit, one, two
            ).astype(BF16)

    out_ref[...] = lax.dot_general(
        dressed[...], slab_ref[...], (((0,), (0,)), ((), ())), preferred_element_type=F32
    )


def contract(blocks, slab):
    return pl.pallas_call(
        contract_kernel,
        grid=(3,),
        out_shape=jax.ShapeDtypeStruct((750, SLAB), F32),
        in_specs=[
            pl.BlockSpec(memory_space=pltpu.VMEM),
            pl.BlockSpec(memory_space=pltpu.VMEM),
        ],
        out_specs=pl.BlockSpec((WIDE, SLAB), lambda m: (m, 0)),
        scratch_shapes=[pltpu.VMEM((1280, WIDE), BF16), pltpu.VMEM((2, 1024, 128), F32)],
        compiler_params=pltpu.CompilerParams(
            dimension_semantics=("arbitrary",), vmem_limit_bytes=32 * 1024 * 1024
        ),
        cost_estimate=pl.CostEstimate(
            flops=2 * 768 * 1280 * SLAB, bytes_accessed=8 * 1024 * 1024, transcendentals=0
        ),
        name="contract",
    )(blocks, slab)


def slab_kernel(slab_ref, out_ref, rows):
    for c in range(8):
        part = slab_ref[:, 128 * c : 128 * (c + 1)].astype(F32)
        rows[8 * c : 8 * c + 8, :] = part[0:8]
        for e in range(2):
            rows[64 + 8 * e + c : 65 + 8 * e + c, :] = part[8 + e : 9 + e]
    out_ref[...] = rows[...].astype(BF16)


def slab_rows(ov_slab):
    return pl.pallas_call(
        slab_kernel,
        out_shape=jax.ShapeDtypeStruct((80, 128), BF16),
        scratch_shapes=[pltpu.VMEM((80, 128), F32)],
        compiler_params=pltpu.CompilerParams(vmem_limit_bytes=4 * 1024 * 1024),
        cost_estimate=pl.CostEstimate(flops=0, bytes_accessed=64 * 1024, transcendentals=0),
        name="slab_rows",
    )(ov_slab)


def round_axis(rows, axis):
    others = [lax.ppermute(rows, axis, [(i, (i + d) % 4) for i in range(4)]) for d in (1, 2, 3)]
    return jnp.concatenate([rows, *others], axis=0)


def shards(vv_vectors, oo_vectors, ov_slab, amplitudes):
    group = ("x_hi", "core")
    quarters = [amplitudes] + [lax.ppermute(amplitudes, group, [(i, i ^ d) for i in range(4)]) for d in (1, 2, 3)]
    rows = round_axis(slab_rows(ov_slab), "z")
    holes = hole_factors(oo_vectors)
    rows, holes, quarters = lax.optimization_barrier((rows, holes, quarters))
    rows = round_axis(rows, "y")
    blocks = dress(vv_vectors, holes, quarters)
    rows, blocks = lax.optimization_barrier((rows, blocks))
    blocks = lax.all_to_all(blocks, RING, split_axis=0, concat_axis=0, tiled=True)
    rows = round_axis(rows, ("x_hi", "x_lo"))
    other = lax.ppermute(rows, "core", [(0, 1), (1, 0)])
    return contract(blocks, ordered(rows.reshape(64, 80, 128), other.reshape(64, 80, 128)))


def solution(mesh):
    split = Mesh(mesh.devices.reshape(2, 2, 4, 4, 2), AXES)
    return jax.shard_map(
        shards,
        mesh=split,
        in_specs=(P(AXES, None, None), P(AXES, None, None), P(AXES, None), P(("x_hi", "core"), None)),
        out_specs=P(AXES, None),
        check_vma=False,
    )
```

time: 90.4 us -> 86.1 us (0.952)
  local copies, waits for them, and re-layouts: 6.59 us -> 2.7 us
  waiting for transfers between devices: 28.4 us -> 29.9 us
  Pallas kernels: 23.7 us -> 22.4 us
    unnamed x9, local copies, waits for them, and re-layouts: 5.57 us -> 2.66 us
    ppermute x1, waiting for transfers between devices: 0.01 us -> 2.66 us  [shards(): other = lax.ppermute(rows, 'core', [(0, 1), (1, 0)])]
    all_to_all x1, waiting for transfers between devices: 20.6 us -> 18.4 us  [shards(): lax.all_to_all(blocks, RING, split_axis=0, concat_axis=0, tiled=True)]
    pallas_call x1 -> x2, Pallas kernels: 4.05 us -> 2.63 us  [the longest x1 2.34 us: ordered(): pl.pallas_call(order_kernel, out_shape=jax.ShapeDtypeStruct((1280, SLAB),...]
    ppermute x9, waiting for transfers between devices: 2.49 us -> 3.64 us  [round_axis(): lax.ppermute(rows, axis, [(i, (i + d) % 4) for i in range(4)])]
    concatenate x1, local copies, waits for them, and re-layouts: 1.02 us -> 0.04 us  [round_axis(): return jnp.concatenate([rows, *others], axis=0)]
  transfers between devices with their start and end apart: 14 -> 14, of which waited for: 5 -> 4; matrix products, arithmetic and copies ran while one was open for 5% -> 0% of each run, Pallas kernels for 20% -> 19%
where the time goes in v3:
time: 86.1 us; the launch traced here: 85.7 us
  starting transfers between devices  30.4 us (35%)
  waiting for transfers between devices  29.9 us (35%)
  Pallas kernels  22.4 us (26%)
  local copies, waits for them, and re-layouts  2.7 us (3%)
    all_to_all x1, waiting for transfers between devices, shards(): lax.all_to_all(blocks, RING, split_axis=0, concat_axis=0, tiled=True)  18.4 us
    pallas_call x1, Pallas kernels, dress(): pl.pallas_call(dress_kernel, out_shape=jax.ShapeDtypeStruct((DEVICES, BLO...  13.9 us
    ppermute x9, starting transfers between devices, round_axis(): lax.ppermute(rows, axis, [(i, (i + d) % 4) for i in range(4)])  11.9 us
    all_to_all x1, starting transfers between devices, shards(): lax.all_to_all(blocks, RING, split_axis=0, concat_axis=0, tiled=True)  9.67 us
    pallas_call x1, Pallas kernels, contract(): pl.pallas_call(contract_kernel, grid=(3,), out_shape=jax.ShapeDtypeStruct...  5.93 us
    ppermute x3, waiting for transfers between devices, shards(): lax.ppermute(amplitudes, group, [(i, i ^ d) for i in range(4)])  5.27 us
    ppermute x3, starting transfers between devices, shards(): lax.ppermute(amplitudes, group, [(i, i ^ d) for i in range(4)])  4.73 us
    ppermute x1, starting transfers between devices, shards(): other = lax.ppermute(rows, 'core', [(0, 1), (1, 0)])  4.18 us
  transfers between devices with their start and end apart: 14, of which 4 were waited for; matrix products, arithmetic and copies ran while one was open for 0% of the time, Pallas kernels for 19%

profile of v3, /device:TPU:1, one launch (start us, length us, event | category | flops | bytes accessed | tf_op | source)
XLA Modules:
  0.0 85.7 jit_solution(3925953909395218905)
XLA Ops:
  0.0 0.0 copy-start.2
  0.0 0.8 copy-done.2
  0.8 4.6 %collective-permute-start.2 = (bf16[80,128]{1,0:T(8,128)(2,1)S(1)}, bf16[80,128]{1,0:T(8,128)(2,1)S(1)}, u32[]{:S(2)}, u32[]{:S(2)}) collective-permute-start(bf16[80,128]{1,0:T(8,128)(2,1)S(1)} %slab_rows.1), channel_id=1, source_target_pairs={{0,24},{8,0},{16,8},{24,16},{1,25},{9,1},{17,9},{25,17},{2,26},{10... | collective-permute-start | bytes 61448 | tf_op jit(solution)/shard_map/ppermute | solution.py:271
  5.4 0.0 collective-permute-start.1
  5.4 0.7 collective-permute-start
  6.1 2.7 %collective-permute-start.4 = (bf16[25,1000]{1,0:T(8,128)(2,1)}, bf16[25,1000]{1,0:T(8,128)(2,1)S(1)}, u32[]{:S(2)}, u32[]{:S(2)}) collective-permute-start(bf16[25,1000]{1,0:T(8,128)(2,1)} %amps_0), channel_id=1, source_target_pairs={{0,64},{32,96},{64,0},{96,32},{1,65},{33,97},{65,1},{97,33},{2,66}... | collective-permute-start | bytes 150008 | tf_op jit(solution)/shard_map/ppermute | solution.py:277
  8.9 1.8 %collective-permute-start.3 = (bf16[25,1000]{1,0:T(8,128)(2,1)}, bf16[25,1000]{1,0:T(8,128)(2,1)S(1)}, u32[]{:S(2)}, u32[]{:S(2)}) collective-permute-start(bf16[25,1000]{1,0:T(8,128)(2,1)} %amps_0), channel_id=1, source_target_pairs={{0,32},{32,0},{64,96},{96,64},{1,33},{33,1},{65,97},{97,65},{2,34}... | collective-permute-start | bytes 150008 | tf_op jit(solution)/shard_map/ppermute | solution.py:277
  10.7 0.0 copy-start
  10.7 0.9 %copy-done = bf16[10,100,100]{2,1,0:T(8,128)(2,1)S(1)} copy-done((bf16[10,100,100]{2,1,0:T(8,128)(2,1)S(1)}, bf16[10,100,100]{2,1,0:T(8,128)(2,1)}, u32[]{:S(2)}) %copy-start) | copy-done | bytes 200024
  11.6 0.3 hole_factors.1.holes_hbm
  11.9 0.0 collective-permute-done.2
  11.9 0.2 collective-permute-start.5
  12.1 0.0 collective-permute-done.1
  12.1 0.0 collective-permute-done
  12.1 0.0 collective-permute-done.4.amps_2
  12.1 0.0 collective-permute-done.3.amps_1
  12.2 5.3 %collective-permute-done.5.amps_3 = bf16[25,1000]{1,0:T(8,128)(2,1)S(1)} collective-permute-done((bf16[25,1000]{1,0:T(8,128)(2,1)}, bf16[25,1000]{1,0:T(8,128)(2,1)S(1)}, u32[]{:S(2)}, u32[]{:S(2)}) %collective-permute-start.5) | collective-permute-done | bytes 50032 | tf_op jit(solution)/shard_map/ppermute | solution.py:277
  17.4 2.7 %collective-permute-start.8 = (bf16[320,128]{1,0:T(8,128)(2,1)S(1)}, bf16[320,128]{1,0:T(8,128)(2,1)S(1)}, u32[]{:S(2)}, u32[]{:S(2)}) collective-permute-start(bf16[320,128]{1,0:T(8,128)(2,1)S(1)} %pad_maximum_fusion.1), channel_id=1, source_target_pairs={{0,6},{2,0},{4,2},{6,4},{1,7},{3,1},{5,3},{7,5},{8,14},{10,8},{12,... | collective-permute-start | bytes 245768 | tf_op jit(solution)/shard_map/ppermute | solution.py:271
  20.2 0.4 collective-permute-start.7
  20.5 0.7 collective-permute-start.6
  21.2 0.0 copy-start.1
  21.2 0.8 copy-done.1
  22.0 13.9 %dress.1 = bf16[128,32,256]{2,1,0:T(8,128)(2,1)} custom-call(bf16[10,1000,1000]{2,1,0:T(8,128)(2,1)} %vv_hbm.1, bf16[10,96,100]{2,1,0:T(8,128)(2,1)S(1)} %hole_factors.1.holes_hbm, bf16[25,1000]{1,0:T(8,128)(2,1)S(1)} %copy-done.1, bf16[25,1000]{1,0:T(8,128)(2,1)S(1)} %collective-permute-done.3.amps_1, bf16[25,1000]{1,0:T(8,128)(2,1)S(1)} %collective-permute-done.4.amps_2, ...), custom_call_target="tpu_custom_call" | custom-call | flops 1920000000 | bytes 20000000 | tf_op jit(solution)/shard_map/dress/pallas_call | solution.py:125
  35.9 0.0 collective-permute-done.8
  35.9 0.0 collective-permute-done.7
  35.9 0.0 collective-permute-done.6
  36.0 0.4 collective-permute-start.9
  36.4 2.4 %collective-permute-start.11 = (bf16[1280,128]{1,0:T(8,128)(2,1)S(1)}, bf16[1280,128]{1,0:T(8,128)(2,1)S(1)}, u32[]{:S(2)}, u32[]{:S(2)}) collective-permute-start(bf16[1280,128]{1,0:T(8,128)(2,1)S(1)} %pad_maximum_fusion), channel_id=1, source_target_pairs={{0,65},{1,0},{64,1},{65,64},{2,67},{3,2},{66,3},{67,66},{4,69},{5,... | collective-permute-start | bytes 983048 | tf_op jit(solution)/shard_map/ppermute | solution.py:271
  38.7 0.0 collective-permute-start.10
  38.7 9.7 %all-to-all-start = ((bf16[128,32,256]{2,1,0:T(8,128)(2,1)}), bf16[128,32,256]{2,1,0:T(8,128)(2,1)}, u32[]{:S(2)}, u32[]{:S(2)}) async-start(bf16[128,32,256]{2,1,0:T(8,128)(2,1)} %dress.1), calls=%async_computation | async-start | bytes 4194304 | tf_op jit(solution)/shard_map/all_to_all | solution.py:284
  48.4 0.0 collective-permute-done.9
  48.5 3.6 %collective-permute-done.10 = bf16[1280,128]{1,0:T(8,128)(2,1)S(1)} collective-permute-done((bf16[1280,128]{1,0:T(8,128)(2,1)S(1)}, bf16[1280,128]{1,0:T(8,128)(2,1)S(1)}, u32[]{:S(2)}, u32[]{:S(2)}) %collective-permute-start.10) | collective-permute-done | bytes 327712 | tf_op jit(solution)/shard_map/ppermute | solution.py:271
  52.2 0.0 collective-permute-done.11
  52.2 4.2 %collective-permute-start.12 = (bf16[5120,128]{1,0:T(8,128)(2,1)S(1)}, bf16[5120,128]{1,0:T(8,128)(2,1)S(1)}, u32[]{:S(2)}, u32[]{:S(2)}) collective-permute-start(bf16[5120,128]{1,0:T(8,128)(2,1)S(1)} %constant_dynamic-update-slice_fusion), channel_id=1, source_target_pairs={{0,32},{32,0},{1,33},{33,1},{2,34},{34,2},{3,35},{35,3},{4,36},{36... | collective-permute-start | bytes 3932168 | tf_op jit(solution)/shard_map/ppermute | solution.py:286
  56.4 2.7 %collective-permute-done.12 = bf16[5120,128]{1,0:T(8,128)(2,1)S(1)} collective-permute-done((bf16[5120,128]{1,0:T(8,128)(2,1)S(1)}, bf16[5120,128]{1,0:T(8,128)(2,1)S(1)}, u32[]{:S(2)}, u32[]{:S(2)}) %collective-permute-start.12) | collective-permute-done | bytes 1310752 | tf_op jit(solution)/shard_map/ppermute | solution.py:286
  59.1 2.3 %ordered.1.slab_ref = bf16[1280,1024]{1,0:T(8,128)(2,1)S(1)} custom-call(bf16[64,80,128]{2,1,0:T(8,128)(2,1)S(1)} %bitcast.2, bf16[64,80,128]{2,1,0:T(8,128)(2,1)S(1)} %bitcast.3), custom_call_target="tpu_custom_call" | custom-call | bytes 6291456 | tf_op jit(solution)/shard_map/ordered/pallas_call | solution.py:177
  61.4 18.4 %all-to-all-done.blocks_ref = bf16[128,32,256]{2,1,0:T(8,128)(2,1)} async-done(((bf16[128,32,256]{2,1,0:T(8,128)(2,1)}), bf16[128,32,256]{2,1,0:T(8,128)(2,1)}, u32[]{:S(2)}, u32[]{:S(2)}) %all-to-all-start) | async-done | bytes 2097184 | tf_op jit(solution)/shard_map/all_to_all | solution.py:284
  79.8 5.9 %contract.1 = f32[750,1024]{1,0:T(8,128)} custom-call(bf16[128,32,256]{2,1,0:T(8,128)(2,1)} %all-to-all-done.blocks_ref, bf16[1280,1024]{1,0:T(8,128)(2,1)S(1)} %ordered.1.slab_ref), custom_call_target="tpu_custom_call" | custom-call | flops 2013265920 | bytes 8388608 | tf_op jit(solution)/shard_map/contract/pallas_call | solution.py:230
  (7 shorter events, 0.2 us)
Async XLA Ops:
  0.0 0.8 copy-start.2
  0.8 11.1 %collective-permute-start.2 = (bf16[80,128]{1,0:T(8,128)(2,1)S(1)}, bf16[80,128]{1,0:T(8,128)(2,1)S(1)}, u32[]{:S(2)}, u32[]{:S(2)}) collective-permute-start(bf16[80,128]{1,0:T(8,128)(2,1)S(1)} %slab_rows.1), channel_id=1, source_target_pairs={{0,24},{8,0},{16,8},{24,16},{1,25},{9,1},{17,9},{25,17},{2,26},{10... | collective-permute-start | bytes 61448 | tf_op jit(solution)/shard_map/ppermute | solution.py:271
  5.4 6.7 %collective-permute-start.1 = (bf16[80,128]{1,0:T(8,128)(2,1)S(1)}, bf16[80,128]{1,0:T(8,128)(2,1)S(1)}, u32[]{:S(2)}, u32[]{:S(2)}) collective-permute-start(bf16[80,128]{1,0:T(8,128)(2,1)S(1)} %slab_rows.1), channel_id=1, source_target_pairs={{0,16},{8,24},{16,0},{24,8},{1,17},{9,25},{17,1},{25,9},{2,18},{10... | collective-permute-start | bytes 61448 | tf_op jit(solution)/shard_map/ppermute | solution.py:271
  5.4 6.7 %collective-permute-start = (bf16[80,128]{1,0:T(8,128)(2,1)S(1)}, bf16[80,128]{1,0:T(8,128)(2,1)S(1)}, u32[]{:S(2)}, u32[]{:S(2)}) collective-permute-start(bf16[80,128]{1,0:T(8,128)(2,1)S(1)} %slab_rows.1), channel_id=1, source_target_pairs={{0,8},{8,16},{16,24},{24,0},{1,9},{9,17},{17,25},{25,1},{2,10},{10... | collective-permute-start | bytes 61448 | tf_op jit(solution)/shard_map/ppermute | solution.py:271
  6.1 6.0 %collective-permute-start.4 = (bf16[25,1000]{1,0:T(8,128)(2,1)}, bf16[25,1000]{1,0:T(8,128)(2,1)S(1)}, u32[]{:S(2)}, u32[]{:S(2)}) collective-permute-start(bf16[25,1000]{1,0:T(8,128)(2,1)} %amps_0), channel_id=1, source_target_pairs={{0,64},{32,96},{64,0},{96,32},{1,65},{33,97},{65,1},{97,33},{2,66}... | collective-permute-start | bytes 150008 | tf_op jit(solution)/shard_map/ppermute | solution.py:277
  8.9 3.3 %collective-permute-start.3 = (bf16[25,1000]{1,0:T(8,128)(2,1)}, bf16[25,1000]{1,0:T(8,128)(2,1)S(1)}, u32[]{:S(2)}, u32[]{:S(2)}) collective-permute-start(bf16[25,1000]{1,0:T(8,128)(2,1)} %amps_0), channel_id=1, source_target_pairs={{0,32},{32,0},{64,96},{96,64},{1,33},{33,1},{65,97},{97,65},{2,34}... | collective-permute-start | bytes 150008 | tf_op jit(solution)/shard_map/ppermute | solution.py:277
  10.7 1.0 %copy-start = (bf16[10,100,100]{2,1,0:T(8,128)(2,1)S(1)}, bf16[10,100,100]{2,1,0:T(8,128)(2,1)}, u32[]{:S(2)}) copy-start(bf16[10,100,100]{2,1,0:T(8,128)(2,1)} %oo_ref.1) | copy-start | bytes 600004
  11.9 5.5 %collective-permute-start.5 = (bf16[25,1000]{1,0:T(8,128)(2,1)}, bf16[25,1000]{1,0:T(8,128)(2,1)S(1)}, u32[]{:S(2)}, u32[]{:S(2)}) collective-permute-start(bf16[25,1000]{1,0:T(8,128)(2,1)} %amps_0), channel_id=1, source_target_pairs={{0,96},{32,64},{64,32},{96,0},{1,97},{33,65},{65,33},{97,1},{2,98}... | collective-permute-start | bytes 150008 | tf_op jit(solution)/shard_map/ppermute | solution.py:277
  17.4 18.5 %collective-permute-start.8 = (bf16[320,128]{1,0:T(8,128)(2,1)S(1)}, bf16[320,128]{1,0:T(8,128)(2,1)S(1)}, u32[]{:S(2)}, u32[]{:S(2)}) collective-permute-start(bf16[320,128]{1,0:T(8,128)(2,1)S(1)} %pad_maximum_fusion.1), channel_id=1, source_target_pairs={{0,6},{2,0},{4,2},{6,4},{1,7},{3,1},{5,3},{7,5},{8,14},{10,8},{12,... | collective-permute-start | bytes 245768 | tf_op jit(solution)/shard_map/ppermute | solution.py:271
  20.2 15.8 %collective-permute-start.7 = (bf16[320,128]{1,0:T(8,128)(2,1)S(1)}, bf16[320,128]{1,0:T(8,128)(2,1)S(1)}, u32[]{:S(2)}, u32[]{:S(2)}) collective-permute-start(bf16[320,128]{1,0:T(8,128)(2,1)S(1)} %pad_maximum_fusion.1), channel_id=1, source_target_pairs={{0,4},{2,6},{4,0},{6,2},{1,5},{3,7},{5,1},{7,3},{8,12},{10,14},{12... | collective-permute-start | bytes 245768 | tf_op jit(solution)/shard_map/ppermute | solution.py:271
  20.5 15.4 %collective-permute-start.6 = (bf16[320,128]{1,0:T(8,128)(2,1)S(1)}, bf16[320,128]{1,0:T(8,128)(2,1)S(1)}, u32[]{:S(2)}, u32[]{:S(2)}) collective-permute-start(bf16[320,128]{1,0:T(8,128)(2,1)S(1)} %pad_maximum_fusion.1), channel_id=1, source_target_pairs={{0,2},{2,4},{4,6},{6,0},{1,3},{3,5},{5,7},{7,1},{8,10},{10,12},{12... | collective-permute-start | bytes 245768 | tf_op jit(solution)/shard_map/ppermute | solution.py:271
  21.2 0.8 copy-start.1
  36.0 12.5 %collective-permute-start.9 = (bf16[1280,128]{1,0:T(8,128)(2,1)S(1)}, bf16[1280,128]{1,0:T(8,128)(2,1)S(1)}, u32[]{:S(2)}, u32[]{:S(2)}) collective-permute-start(bf16[1280,128]{1,0:T(8,128)(2,1)S(1)} %pad_maximum_fusion), channel_id=1, source_target_pairs={{0,1},{1,64},{64,65},{65,0},{2,3},{3,66},{66,67},{67,2},{4,5},{5,6... | collective-permute-start | bytes 983048 | tf_op jit(solution)/shard_map/ppermute | solution.py:271
  36.4 15.8 %collective-permute-start.11 = (bf16[1280,128]{1,0:T(8,128)(2,1)S(1)}, bf16[1280,128]{1,0:T(8,128)(2,1)S(1)}, u32[]{:S(2)}, u32[]{:S(2)}) collective-permute-start(bf16[1280,128]{1,0:T(8,128)(2,1)S(1)} %pad_maximum_fusion), channel_id=1, source_target_pairs={{0,65},{1,0},{64,1},{65,64},{2,67},{3,2},{66,3},{67,66},{4,69},{5,... | collective-permute-start | bytes 983048 | tf_op jit(solution)/shard_map/ppermute | solution.py:271
  38.7 13.4 %collective-permute-start.10 = (bf16[1280,128]{1,0:T(8,128)(2,1)S(1)}, bf16[1280,128]{1,0:T(8,128)(2,1)S(1)}, u32[]{:S(2)}, u32[]{:S(2)}) collective-permute-start(bf16[1280,128]{1,0:T(8,128)(2,1)S(1)} %pad_maximum_fusion), channel_id=1, source_target_pairs={{0,64},{1,65},{64,0},{65,1},{2,66},{3,67},{66,2},{67,3},{4,68},{5,... | collective-permute-start | bytes 983048 | tf_op jit(solution)/shard_map/ppermute | solution.py:271
  38.7 41.1 %all-to-all-start = ((bf16[128,32,256]{2,1,0:T(8,128)(2,1)}), bf16[128,32,256]{2,1,0:T(8,128)(2,1)}, u32[]{:S(2)}, u32[]{:S(2)}) async-start(bf16[128,32,256]{2,1,0:T(8,128)(2,1)} %dress.1), calls=%async_computation | async-start | bytes 4194304 | tf_op jit(solution)/shard_map/all_to_all | solution.py:284
  52.2 6.8 %collective-permute-start.12 = (bf16[5120,128]{1,0:T(8,128)(2,1)S(1)}, bf16[5120,128]{1,0:T(8,128)(2,1)S(1)}, u32[]{:S(2)}, u32[]{:S(2)}) collective-permute-start(bf16[5120,128]{1,0:T(8,128)(2,1)S(1)} %constant_dynamic-update-slice_fusion), channel_id=1, source_target_pairs={{0,32},{32,0},{1,33},{33,1},{2,34},{34,2},{3,35},{35,3},{4,36},{36... | collective-permute-start | bytes 3932168 | tf_op jit(solution)/shard_map/ppermute | solution.py:286
